TPU v7x, 32 devices: a whole 2x2x4 slice. The times are simulated.
32 devices in a mesh: gx: 8 (over y, x, core), gy: 4 (over z).
Axes of the slice: x: 2, y: 2, z: 4, core: 2. Of those that a mesh axis runs over, the one named last changes fastest.
Arguments:
- resid: bfloat16 [128, 16384], P(('gx', 'gy')), may hold values from -6 to 6
- query: bfloat16 [128, 16384], P(('gx', 'gy')), may hold values from -6 to 6
- key_new: bfloat16 [128, 1024], P(('gx', 'gy')), may hold values from -6 to 6
- value_new: bfloat16 [128, 1024], P(('gx', 'gy')), may hold values from -6 to 6
- cache_keys: bfloat16 [128, 128, 1024], P(('gx', 'gy'))
- cache_values: bfloat16 [128, 128, 1024], P(('gx', 'gy')), may hold values from -6 to 6
- lengths: int32 [128], P(('gx', 'gy')), may hold values from 1 to 128, as said below
- norm_gain: bfloat16 [16384], replicated, may hold values from 0.5 to 1.5
- gate_weight: bfloat16 [16384, 26624], P('gx', 'gy'), may hold values from -0.046875 to 0.046875
- up_weight: bfloat16 [16384, 26624], P('gx', 'gy'), may hold values from -0.046875 to 0.046875
- down_weight: bfloat16 [26624, 16384], P('gy', 'gx'), may hold values from -0.0390625 to 0.0390625
Outputs:
- layer_out: bfloat16 [128, 16384], P(('gx', 'gy'))
Inputs may be any that keep to these rules, and one draw needn't show every extreme that they name: `lengths`: some row has all 128 positions live.
All inputs are finite; a program needn't handle non-finite values.
Results may differ from a plain program's by a relative error of at most 0.0057.
Values may be sent and summed in bfloat16 or wider, within the bound.
A program may use at most 192 MiB of HBM per device.

v0:
```python
import jax
import jax.numpy as jnp
from jax import lax
from jax.sharding import PartitionSpec as P

HQ = 128
KV = 8
HD = 128


def attend_row(query, key_new, value_new, cache_keys, cache_values, length):
    scale_factor = HD ** (-0.5)
    span = cache_keys.shape[0]
    heads = query.astype(jnp.float32).reshape(KV, HQ // KV, HD)
    keys = cache_keys.reshape(span, KV, HD)
    values = cache_values.reshape(span, KV, HD)
    knew = key_new.astype(jnp.float32).reshape(KV, HD)
    vnew = value_new.astype(jnp.float32).reshape(KV, HD)
    scores = (
        jnp.einsum(
            "kgd,pkd->kgp",
            query.reshape(KV, HQ // KV, HD),
            keys,
            preferred_element_type=jnp.float32,
        )
        * scale_factor
    )
    places = jnp.arange(span, dtype=jnp.int32)
    scores = jnp.where(places[None, None, :] < length, scores, jnp.float32(-1e30))
    own = jnp.einsum("kgd,kd->kg", heads, knew) * scale_factor
    top = jnp.maximum(jnp.max(scores, axis=-1), own)
    expo = jnp.exp(scores - top[..., None])
    own_expo = jnp.exp(own - top)
    total = jnp.sum(expo, axis=-1) + own_expo
    probs = (expo / total[..., None]).astype(jnp.bfloat16)
    own_prob = (own_expo / total).astype(jnp.bfloat16).astype(jnp.float32)
    mixed = (
        jnp.einsum("kgp,pkd->kgd", probs, values, preferred_element_type=jnp.float32)
        + own_prob[..., None] * vnew[:, None, :]
    )
    return mixed.reshape(HQ * HD)


def on_device(
    resid,
    query,
    key_new,
    value_new,
    cache_keys,
    cache_values,
    lengths,
    norm_gain,
    gate_weight,
    up_weight,
    down_weight,
):
    attended = jax.vmap(attend_row)(query, key_new, value_new, cache_keys, cache_values, lengths)
    mid = (resid.astype(jnp.float32) + attended).astype(jnp.bfloat16)
    midf = mid.astype(jnp.float32)
    inverse = lax.rsqrt(jnp.mean(midf * midf, axis=-1, keepdims=True) + 1e-05)
    normed = (midf * inverse * norm_gain.astype(jnp.float32)).astype(jnp.bfloat16)
    stacked = jnp.stack([mid, normed], axis=1)
    blocks = lax.all_to_all(stacked, "gx", split_axis=2, concat_axis=0, tiled=True)
    gathered = lax.all_gather(blocks, "gy", axis=0, tiled=True)
    mid_rows = gathered[:, 0, :]
    normed_rows = gathered[:, 1, :]
    gate_part = jnp.dot(normed_rows, gate_weight, preferred_element_type=jnp.float32)
    up_part = jnp.dot(normed_rows, up_weight, preferred_element_type=jnp.float32)
    gate, up = lax.psum((gate_part, up_part), "gx")
    act = (jax.nn.silu(gate) * up).astype(jnp.bfloat16)
    block_rows = act.shape[0] // lax.axis_size("gy")
    ffn = lax.psum_scatter(
        jnp.dot(act, down_weight, preferred_element_type=jnp.float32),
        "gy",
        scatter_dimension=0,
        tiled=True,
    )
    own_mid = lax.dynamic_slice_in_dim(mid_rows, lax.axis_index("gy") * block_rows, block_rows, 0)
    finished = (own_mid.astype(jnp.float32) + ffn).astype(jnp.bfloat16)
    return lax.all_to_all(finished, "gx", split_axis=0, concat_axis=1, tiled=True)


def solution(mesh):
    placed = (
        P(("gx", "gy"), None),
        P(("gx", "gy"), None),
        P(("gx", "gy"), None),
        P(("gx", "gy"), None),
        P(("gx", "gy"), None, None),
        P(("gx", "gy"), None, None),
        P(("gx", "gy")),
        P(),
        P("gx", "gy"),
        P("gx", "gy"),
        P("gy", "gx"),
    )
    return jax.shard_map(
        on_device, mesh=mesh, in_specs=placed, out_specs=P(("gx", "gy"), None), check_vma=False
    )
```

profile of v0, /device:TPU:0, one launch (start us, length us, event | category | flops | bytes accessed | tf_op | source)
XLA Modules:
  0.0 320.8 jit_solution(10934704975294698136)
XLA Ops:
  6.5 0.0 copy-start
  6.5 0.0 copy-start.3
  6.5 0.0 all-gather.2.cloned.1.call-start
  6.5 0.8 iota_compare_fusion
  7.4 0.7 reshape.67
  8.1 0.7 convert_bitcast_fusion
  8.8 0.8 convert_element_type.45
  9.5 0.9 copy.32
  10.5 0.2 fusion.23
  10.6 0.0 copy-done
  10.7 0.7 fusion.22
  11.4 0.3 fusion.14
  11.7 1.7 convolution_add_fusion
  13.4 0.0 copy-done.3
  13.4 0.3 fusion.9
  13.7 0.1 fusion.15
  13.9 0.2 pad_maximum_fusion
  14.1 13.1 %copy.25 = bf16[4,2,16384]{0,1,2:T(2,128)(2,1)} copy(bf16[4,2,16384]{2,0,1:T(4,128)(2,1)S(1)} %pad_maximum_fusion) | data formatting | bytes 524288 | tf_op jit(solution)/shard_map/stack | solution.py:62
  27.2 16.2 %reshape.68 = bf16[8,2,8192]{2,1,0:T(2,128)(2,1)S(1)} reshape(bf16[16384,2,4]{2,1,0:T(2,128)(2,1)} %bitcast.58) | data formatting | bytes 524288
  43.4 11.9 %all_to_all.37 = bf16[8,2,8192]{2,1,0:T(2,128)(2,1)S(1)} all-to-all(bf16[8,2,8192]{2,1,0:T(2,128)(2,1)S(1)} %reshape.68), channel_id=1, replica_groups=mesh['gx'=8,'gy'=4] {'gx'}, dimensions={0} | all-to-all | bytes 524288 | tf_op jit(solution)/shard_map/all_to_all | solution.py:63
  55.3 19.1 %reshape.69 = bf16[16384,2,4]{2,1,0:T(2,128)(2,1)} reshape(bf16[8,2,8192]{2,1,0:T(2,128)(2,1)S(1)} %all_to_all.37) | data formatting | bytes 524288
  74.3 19.2 %copy.26 = bf16[4,2,8,2048]{3,0,2,1:T(4,128)(2,1)S(1)} copy(bf16[4,2,8,2048]{0,1,3,2:T(2,128)(2,1)} %bitcast.59) | data formatting | bytes 524288 | tf_op jit(solution)/shard_map/all_to_all | solution.py:63
  93.5 0.8 all_to_all.30
  94.3 0.0 all-gather.2.cloned.1.call-update
  94.3 0.2 all-reduce.3.cloned.1.call-start
  94.5 27.2 %all-gather.2.cloned.1.call-done = bf16[128,2,2048]{2,0,1:T(8,128)(2,1)} async-done(((bf16[32,2,2048]{2,0,1:T(8,128)(2,1)}), bf16[128,2,2048]{2,0,1:T(8,128)(2,1)}) %all-gather.2.cloned.1.call-update) | async-done | bytes 1048592 | tf_op jit(solution)/shard_map/all_gather | solution.py:64
  121.8 0.0 copy-start.2
  121.8 14.5 %fusion.7 = f32[128,6656]{1,0:T(8,128)} fusion(bf16[2048,6656]{1,0:T(8,128)(2,1)} %param.20, bf16[128,2,2048]{2,0,1:T(8,128)(2,1)} %all-gather.2.cloned.1.call-done), kind=kOutput, calls=%fused_computation.11 | convolution fusion | flops 3489660928 | bytes 31195136 | tf_op jit(solution)/shard_map/dot_general | solution.py:68
  136.3 0.0 copy-done.2
  136.3 14.3 %fusion.8 = f32[128,6656]{1,0:T(8,128)} fusion(bf16[2048,6656]{1,0:T(8,128)(2,1)} %param.19, bf16[128,2,2048]{2,0,1:T(8,128)(2,1)S(1)} %copy-done.2), kind=kOutput, calls=%fused_computation.12 | convolution fusion | flops 3489660928 | bytes 31195136 | tf_op jit(solution)/shard_map/dot_general | solution.py:67
  150.6 0.0 all-reduce.3.cloned.1.call-update
  150.6 0.0 reduce-scatter.2.cloned.1.call-start
  150.6 109.8 %all-reduce.3.cloned.1.call-done = (f32[128,6656]{1,0:T(8,128)}, f32[128,6656]{1,0:T(8,128)}) async-done(((f32[128,6656]{1,0:T(8,128)}, f32[128,6656]{1,0:T(8,128)}), (f32[128,6656]{1,0:T(8,128)}, f32[128,6656]{1,0:T(8,128)})) %all-reduce.3.cloned.1.call-update) | async-done | bytes 6815760 | tf_op jit(solution)/shard_map/psum | solution.py:69
  260.4 0.0 slice-start
  260.4 0.0 copy-start.1
  260.4 15.7 %fusion = f32[128,2048]{1,0:T(8,128)} fusion(bf16[6656,2048]{1,0:T(8,128)(2,1)} %param.21, f32[128,6656]{1,0:T(8,128)} %get-tuple-element.5, f32[128,6656]{1,0:T(8,128)} %get-tuple-element.6), kind=kOutput, calls=%fused_computation.1 | convolution fusion | flops 3494772736 | bytes 35127296 | tf_op jit(solution)/shard_map/dot_general | solution.py:73
  276.2 0.0 reduce-scatter.2.cloned.1.call-update
  276.2 27.4 %reduce-scatter.2.cloned.1.call-done = f32[32,2048]{1,0:T(8,128)} async-done(((f32[128,2048]{1,0:T(8,128)}), f32[32,2048]{1,0:T(8,128)}) %reduce-scatter.2.cloned.1.call-update) | async-done | bytes 262160 | tf_op jit(solution)/shard_map/reduce_scatter | solution.py:72
  303.6 0.0 slice-done
  303.6 1.0 fusion.13
  304.6 0.1 all_to_all.31
  304.6 9.0 %all_to_all.38 = bf16[8,4,2048]{2,1,0:T(4,128)(2,1)S(1)} all-to-all(bf16[8,4,2048]{2,1,0:T(4,128)(2,1)S(1)} %all_to_all.31), channel_id=1, replica_groups=mesh['gx'=8,'gy'=4] {'gx'}, dimensions={0} | all-to-all | bytes 262144 | tf_op jit(solution)/shard_map/all_to_all | solution.py:80
  313.6 0.7 copy.52
  314.3 0.0 copy-done.1
  (4 shorter events, 0.0 us)
Async XLA Ops:
  6.5 4.1 %copy-start = (bf16[4,128,1024]{2,1,0:T(8,128)(2,1)S(1)}, bf16[4,128,1024]{2,1,0:T(8,128)(2,1)}, u32[]{:S(2)}) copy-start(bf16[4,128,1024]{2,1,0:T(8,128)(2,1)} %param.15) | copy-start | bytes 3145732
  6.5 6.8 %copy-start.3 = (bf16[4,16384]{1,0:T(4,128)(2,1)S(1)}, bf16[4,16384]{1,0:T(4,128)(2,1)}, u32[]{:S(2)}) copy-start(bf16[4,16384]{1,0:T(4,128)(2,1)} %param.11) | copy-start | bytes 393220
  6.5 115.2 %all-gather.2.cloned.1.call-start = ((), (), s32[]{:S(2)}) async-start(), calls=%async_computation.3 | async-start | bytes 1310720 | tf_op jit(solution)/shard_map/all_gather | solution.py:64
  94.3 166.1 %all-reduce.3.cloned.1.call-start = ((), (), s32[]{:S(2)}) async-start(), calls=%async_computation.5 | async-start | bytes 13631488 | tf_op jit(solution)/shard_map/psum | solution.py:69
  121.8 14.5 %copy-start.2 = (bf16[128,2,2048]{2,0,1:T(8,128)(2,1)S(1)}, bf16[128,2,2048]{2,0,1:T(8,128)(2,1)}, u32[]{:S(2)}) copy-start(bf16[128,2,2048]{2,0,1:T(8,128)(2,1)} %all-gather.2.cloned.1.call-done) | copy-start | bytes 3145732
  150.6 153.0 %reduce-scatter.2.cloned.1.call-start = ((), (), s32[]{:S(2)}) async-start(), calls=%async_computation.4 | async-start | bytes 1310720 | tf_op jit(solution)/shard_map/reduce_scatter | solution.py:72
  260.4 43.2 %slice-start = ((bf16[128,2,2048]{2,0,1:T(8,128)(2,1)}), bf16[128,1,2048]{2,0,1:T(8,128)(2,1)S(1)}, s32[]{:S(2)}) async-start(bf16[128,2,2048]{2,0,1:T(8,128)(2,1)} %all-gather.2.cloned.1.call-done), calls=%async_computation.6 | async-start | bytes 1048576 | tf_op jit(solution)/shard_map/slice | solution.py:65
  260.4 53.9 %copy-start.1 = (bf16[4,128,1024]{2,1,0:T(8,128)(2,1)S(1)}, bf16[4,128,1024]{2,1,0:T(8,128)(2,1)}, u32[]{:S(2)}) copy-start(bf16[4,128,1024]{2,1,0:T(8,128)(2,1)} %param.15) | copy-start | bytes 3145732
Sparse Core Ops, SparseCore 0:
  94.4 27.2 all-gather.1
  150.7 109.6 all-reduce.2
  276.3 27.2 reduce-scatter.1
where the time goes:
time: 322 us; the launch traced here: 321 us
  waiting for transfers between devices  164 us (51%)
  local copies, waits for them, and re-layouts  70.7 us (22%)
  matrix products  47.1 us (15%)
  blocking collectives  20.9 us (6%)
  between operations  13.2 us (4%)
  other arithmetic  4.23 us (1%)
    psum x1, waiting for transfers between devices, on_device(): gate, up = lax.psum((gate_part, up_part), 'gx')  110 us
    unnamed x13, local copies, waits for them, and re-layouts  36.9 us
    reduce_scatter x1, waiting for transfers between devices, on_device(): lax.psum_scatter(jnp.dot(act, down_weight, preferred_element_type=jnp.flo...  27.4 us
    all_gather x1, waiting for transfers between devices, on_device(): gathered = lax.all_gather(blocks, 'gy', axis=0, tiled=True)  27.2 us
    all_to_all x2, local copies, waits for them, and re-layouts, on_device(): lax.all_to_all(stacked, 'gx', split_axis=2, concat_axis=0, tiled=True)  20 us
    dot_general x1, matrix products, on_device(): jnp.dot(act, down_weight, preferred_element_type=jnp.float32)  15.7 us
    dot_general x1, matrix products, on_device(): jnp.dot(normed_rows, up_weight, preferred_element_type=jnp.float32)  14.5 us
    dot_general x1, matrix products, on_device(): jnp.dot(normed_rows, gate_weight, preferred_element_type=jnp.float32)  14.3 us
  transfers between devices with their start and end apart: 3, of which 3 were waited for; matrix products, arithmetic and copies ran while one was open for 0% of the time, Pallas kernels for 0%

commit v1 on v0

v1 whole, which is shorter than its diff:
```python
import functools

import jax
import jax.numpy as jnp
from jax import lax
from jax.experimental import pallas as pl
from jax.experimental.pallas import tpu as pltpu
from jax.sharding import PartitionSpec as P

KV = 8
HD = 128
MESH = pl.DeviceIdType.MESH
F32 = jnp.float32
BF16 = jnp.bfloat16


def kernel(
    cfg,
    lengths,
    resid,
    query,
    key_new,
    value_new,
    gain,
    cache_keys,
    cache_values,
    gate_hbm,
    up_hbm,
    down_hbm,
    out,
    kbuf,
    vbuf,
    mid,
    nbuf,
    xbuf,
    xs,
    gbuf,
    ubuf,
    dbuf,
    sums,
    recvs,
    agbuf,
    acc,
    obuf,
    rbuf,
    cache_sem,
    gate_sem,
    up_sem,
    down_sem,
    x_send,
    x_recv,
    o_send,
    o_recv,
    rs_send,
    rs_recv,
    ag_send,
    ag_recv,
):
    X, Y, K, C, NC, SG, SD = cfg
    n = X * Y
    gi, gj = lax.axis_index("gx"), lax.axis_index("gy")
    me = gi * Y + gj
    rloc, D = resid.shape
    span = cache_keys.shape[1]
    Dk = D // X
    N = xs.shape[0]
    G = D // (KV * HD)
    bits = [(gi // 2**s) % 2 for s in range(K)]
    partner = [gi + (1 - 2 * bits[s]) * 2**s for s in range(K)]

    barrier = pltpu.get_barrier_semaphore()

    @pl.loop(1, n)
    def _(d):
        t = (me + d) % n
        pl.semaphore_signal(barrier, inc=1, device_id=(t // Y, t % Y), device_id_type=MESH)

    kcopy = pltpu.make_async_copy(cache_keys, kbuf, cache_sem.at[0])
    vcopy = pltpu.make_async_copy(cache_values, vbuf, cache_sem.at[1])
    kcopy.start()
    vcopy.start()

    def gate_copy(c):
        cols = pl.ds(pl.multiple_of(c * C, C), C)
        return pltpu.make_async_copy(gate_hbm.at[:, cols], gbuf.at[c % SG], gate_sem.at[c % SG])

    def up_copy(c):
        cols = pl.ds(pl.multiple_of(c * C, C), C)
        return pltpu.make_async_copy(up_hbm.at[:, cols], ubuf.at[c % SG], up_sem.at[c % SG])

    def down_copy(c):
        rows = pl.ds(pl.multiple_of(c * C, C), C)
        return pltpu.make_async_copy(down_hbm.at[rows, :], dbuf.at[c % SD], down_sem.at[c % SD])

    @pl.loop(0, SG)
    def _(c):
        gate_copy(c).start()
        up_copy(c).start()

    @pl.loop(0, SD)
    def _(c):
        down_copy(c).start()

    M, S = G * rloc, rloc * span
    col = lax.broadcasted_iota(jnp.int32, (M, S), 1)
    row = lax.broadcasted_iota(jnp.int32, (M, S), 0) % rloc
    limit = jnp.zeros((M, S), jnp.int32)
    for r in range(rloc):
        limit = jnp.where(row == r, r * span + lengths[r], limit)
    live = (col >= row * span) & (col < limit)
    kcopy.wait()
    vcopy.wait()
    scale = HD ** (-0.5)

    def head(k, square):
        wide = pl.ds(pl.multiple_of(k * G * HD, G * HD), G * HD)
        one = pl.ds(pl.multiple_of(k * HD, HD), HD)
        q = query[:, wide].astype(F32)
        q = jnp.concatenate([q[:, g * HD : (g + 1) * HD] for g in range(G)], axis=0)
        kn = jnp.concatenate([key_new[:, one].astype(F32)] * G, axis=0)
        vn = jnp.concatenate([value_new[:, one].astype(F32)] * G, axis=0)
        keys = kbuf[:, :, one].reshape(S, HD)
        values = vbuf[:, :, one].reshape(S, HD)
        s = lax.dot_general(
            q.astype(BF16), keys, (((1,), (1,)), ((), ())), preferred_element_type=F32
        )
        s = jnp.where(live, s * scale, -1e30)
        own = jnp.sum(q * kn, axis=1, keepdims=True) * scale
        top = jnp.maximum(jnp.max(s, axis=1, keepdims=True), own)
        e = jnp.where(live, jnp.exp(s - top), 0.0)
        eo = jnp.exp(own - top)
        total = jnp.sum(e, axis=1, keepdims=True) + eo
        p = (e / total).astype(BF16)
        po = (eo / total).astype(BF16).astype(F32)
        mixed = jnp.dot(p, values, preferred_element_type=F32) + po * vn
        att = jnp.concatenate([mixed[g * rloc : (g + 1) * rloc] for g in range(G)], axis=1)
        m = (resid[:, wide].astype(F32) + att).astype(BF16)
        mid[:, wide] = m
        mf = m.astype(F32)
        return square + jnp.sum(mf * mf, axis=1, keepdims=True)

    square = lax.fori_loop(0, KV, head, jnp.zeros((rloc, 1), F32))
    inverse = lax.rsqrt(square / D + 1e-05)

    @pl.loop(0, X)
    def _(i):
        part = pl.ds(pl.multiple_of(i * Dk, Dk), Dk)
        nbuf[i] = (mid[:, part].astype(F32) * inverse * gain[:, part].astype(F32)).astype(BF16)

    xbuf[me] = nbuf[gi]
    pl.semaphore_wait(barrier, n - 1)

    @pl.loop(1, n)
    def _(d):
        t = (me + d) % n
        pltpu.make_async_remote_copy(
            src_ref=nbuf.at[t // Y],
            dst_ref=xbuf.at[me],
            send_sem=x_send,
            recv_sem=x_recv,
            device_id=(t // Y, t % Y),
            device_id_type=MESH,
        ).start()

    acc[...] = jnp.zeros_like(acc)
    pltpu.make_async_copy(xbuf.at[pl.ds(0, n - 1)], xbuf.at[pl.ds(0, n - 1)], x_recv).wait()
    per = 16 // rloc

    @pl.loop(0, N // 16)
    def _(b):
        rows = [xbuf[b * per + a].astype(F32) for a in range(per)]
        xs[pl.ds(pl.multiple_of(b * 16, 16), 16), :] = jnp.concatenate(rows, axis=0).astype(BF16)

    ALL = slice(None)

    def rs_copy(s, c):
        return pltpu.make_async_remote_copy(
            src_ref=sums[s].at[(c,) + (ALL,) * (K - s - 1) + (1 - bits[s],)],
            dst_ref=recvs[s].at[c],
            send_sem=rs_send.at[s],
            recv_sem=rs_recv.at[s, c],
            device_id=(partner[s], gj),
            device_id_type=MESH,
        )

    order = list(range(1, K)) + [0]

    def ag_copy(a, c, incoming=False):
        done = order[:a]
        idx = (c,)
        for b in range(K - 1, -1, -1):
            if b in done:
                idx += (ALL,)
            elif b == order[a] and incoming:
                idx += (1 - bits[b],)
            else:
                idx += (bits[b],)
        return pltpu.make_async_remote_copy(
            src_ref=agbuf.at[idx],
            dst_ref=agbuf.at[idx],
            send_sem=ag_send.at[a],
            recv_sem=ag_recv.at[a, c],
            device_id=(partner[order[a]], gj),
            device_id_type=MESH,
        )

    def stage_matmul(c):
        gate_copy(c).wait()
        x = xs[...]
        shape = (2,) * K + (N // X, C)
        g = jnp.dot(x, gbuf[c % SG], preferred_element_type=F32)
        sums[0][(c,) + (ALL,) * (K + 1) + (pl.ds(0, C),)] = g.astype(BF16).reshape(shape)
        up_copy(c).wait()
        u = jnp.dot(x, ubuf[c % SG], preferred_element_type=F32)
        sums[0][(c,) + (ALL,) * (K + 1) + (pl.ds(C, C),)] = u.astype(BF16).reshape(shape)
        rs_copy(0, c).start()

        @pl.when(c + SG < NC)
        def _():
            gate_copy(c + SG).start()
            up_copy(c + SG).start()

    def stage_reduce(s, c):
        rs_copy(s - 1, c).wait_recv()
        kept = sums[s - 1][(c,) + (ALL,) * (K - s) + (bits[s - 1],)].astype(F32)
        v = kept + recvs[s - 1][c].astype(F32)
        if s < K:
            sums[s][c] = v.astype(BF16)
            rs_copy(s, c).start()
        else:
            gate, up = v[:, :C], v[:, C:]
            act = gate / (1.0 + jnp.exp(-gate)) * up
            agbuf[(c,) + tuple(bits[b] for b in range(K - 1, -1, -1))] = act.astype(BF16)
            ag_copy(0, c).start()

    def stage_gather(a, c):
        ag_copy(a - 1, c, True).wait_recv()
        ag_copy(a, c).start()

    NW = min(512, Dk)

    def stage_down(c):
        ag_copy(K - 1, c, True).wait_recv()
        down_copy(c).wait()
        act = agbuf[c].reshape(N, C)
        for w in range(Dk // NW):
            cols = pl.ds(w * NW, NW)
            acc[:, cols] += jnp.dot(act, dbuf[c % SD, :, cols], preferred_element_type=F32)

        @pl.when(c + SD < NC)
        def _():
            down_copy(c + SD).start()

    stages = [stage_matmul]
    stages += [functools.partial(stage_reduce, s) for s in range(1, K + 1)]
    stages += [functools.partial(stage_gather, a) for a in range(1, K)]
    stages += [stage_down]

    @pl.loop(0, NC + len(stages) - 1)
    def _(t):
        for s, stage in enumerate(stages):
            c = t - s

            @pl.when((c >= 0) & (c < NC))
            def _():
                stage(c)

    @pl.loop(0, N // 8)
    def _(b):
        v = acc[pl.ds(pl.multiple_of(b * 8, 8), 8), :].astype(BF16)
        for a in range(8 // rloc):
            obuf[b * (8 // rloc) + a] = v[a * rloc : (a + 1) * rloc]

    @pl.loop(1, n)
    def _(d):
        t = (me + d) % n
        pltpu.make_async_remote_copy(
            src_ref=obuf.at[t],
            dst_ref=rbuf.at[me],
            send_sem=o_send,
            recv_sem=o_recv,
            device_id=(t // Y, t % Y),
            device_id_type=MESH,
        ).start()

    rbuf[me] = obuf[me]
    pltpu.make_async_copy(rbuf.at[pl.ds(0, n - 1)], rbuf.at[pl.ds(0, n - 1)], o_recv).wait()

    @pl.loop(0, X)
    def _(i):
        part = pl.ds(pl.multiple_of(i * Dk, Dk), Dk)
        v = rbuf[i * Y].astype(F32)
        for j in range(1, Y):
            v += rbuf[i * Y + j].astype(F32)
        out[:, part] = (mid[:, part].astype(F32) + v).astype(BF16)

    pltpu.make_async_copy(xbuf.at[pl.ds(0, n - 1)], xbuf.at[pl.ds(0, n - 1)], x_send).wait()
    pltpu.make_async_copy(rbuf.at[pl.ds(0, n - 1)], rbuf.at[pl.ds(0, n - 1)], o_send).wait()
    for s in range(K):
        pltpu.make_async_copy(recvs[s], recvs[s], rs_send.at[s]).wait()
    for a in range(K):
        idx = (ALL,)
        for b in range(K - 1, -1, -1):
            idx += (ALL,) if b in order[:a] else (bits[b],)
        pltpu.make_async_copy(agbuf.at[idx], agbuf.at[idx], ag_send.at[a]).wait()


def pick_chunk(width):
    c = 512
    while width % c:
        c //= 2
    return c


def on_device(
    X,
    Y,
    resid,
    query,
    key_new,
    value_new,
    cache_keys,
    cache_values,
    lengths,
    norm_gain,
    gate_weight,
    up_weight,
    down_weight,
):
    rloc, D = resid.shape
    n = X * Y
    N = rloc * n
    K = X.bit_length() - 1
    Dk, F = gate_weight.shape
    C = pick_chunk(F)
    NC = F // C
    SG, SD = min(7, NC), min(6, NC)
    R = N // X
    sums = [pltpu.VMEM((NC,) + (2,) * (K - s) + (R, 2 * C), BF16) for s in range(K)]
    recvs = [pltpu.VMEM((NC,) + (2,) * (K - s - 1) + (R, 2 * C), BF16) for s in range(K)]
    DMA = pltpu.SemaphoreType.DMA
    vmem = pl.BlockSpec(memory_space=pltpu.VMEM)
    hbm = pl.BlockSpec(memory_space=pl.ANY)
    scratch = [
        pltpu.VMEM(cache_keys.shape, BF16),
        pltpu.VMEM(cache_values.shape, BF16),
        pltpu.VMEM((rloc, D), BF16),
        pltpu.VMEM((X, rloc, Dk), BF16),
        pltpu.VMEM((n, rloc, Dk), BF16),
        pltpu.VMEM((N, Dk), BF16),
        pltpu.VMEM((SG, Dk, C), BF16),
        pltpu.VMEM((SG, Dk, C), BF16),
        pltpu.VMEM((SD, C, Dk), BF16),
        sums,
        recvs,
        pltpu.VMEM((NC,) + (2,) * K + (R, C), BF16),
        pltpu.VMEM((N, Dk), F32),
        pltpu.VMEM((n, rloc, Dk), BF16),
        pltpu.VMEM((n, rloc, Dk), BF16),
        DMA((2,)),
        DMA((SG,)),
        DMA((SG,)),
        DMA((SD,)),
        DMA,
        DMA,
        DMA,
        DMA,
        DMA((K,)),
        DMA((K, NC)),
        DMA((K,)),
        DMA((K, NC)),
    ]
    return pl.pallas_call(
        functools.partial(kernel, (X, Y, K, C, NC, SG, SD)),
        out_shape=jax.ShapeDtypeStruct((rloc, D), BF16),
        in_specs=[pl.BlockSpec(memory_space=pltpu.SMEM)] + [vmem] * 5 + [hbm] * 5,
        out_specs=vmem,
        scratch_shapes=scratch,
        compiler_params=pltpu.CompilerParams(
            collective_id=0, has_side_effects=True, vmem_limit_bytes=62 << 20
        ),
        name="layer",
    )(
        lengths,
        resid,
        query,
        key_new,
        value_new,
        norm_gain.reshape(1, D),
        cache_keys,
        cache_values,
        gate_weight,
        up_weight,
        down_weight,
    )


def solution(mesh):
    rows = P(("gx", "gy"), None)
    placed = (rows,) * 4 + (P(("gx", "gy"), None, None),) * 2
    placed += (P(("gx", "gy")), P(), P("gx", "gy"), P("gx", "gy"), P("gy", "gx"))
    return jax.shard_map(
        functools.partial(on_device, mesh.shape["gx"], mesh.shape["gy"]),
        mesh=mesh,
        in_specs=placed,
        out_specs=rows,
        check_vma=False,
    )
```

time: 322 us -> 90.4 us (0.28)
  waiting for transfers between devices: 164 us -> 0 us
  Pallas kernels: 0 us -> 87.2 us
  local copies, waits for them, and re-layouts: 70.7 us -> 3.03 us
  matrix products: 47.1 us -> 0 us
  blocking collectives: 20.9 us -> 0 us
  between operations: 13.2 us -> 0.01 us
  other arithmetic: 4.23 us -> 0 us
    psum x1 -> x0, waiting for transfers between devices: 110 us -> none  [on_device(): gate, up = lax.psum((gate_part, up_part), 'gx')]
    pallas_call x0 -> x1, Pallas kernels: none -> 87.2 us  [on_device(): pl.pallas_call(functools.partial(kernel, (X, Y, K, C, NC, SG, SD)), out_s...]
    dot_general x6 -> x0, matrix products: 47.1 us -> none  [the longest x1 15.7 us: on_device(): jnp.dot(act, down_weight, preferred_element_type=jnp.float32)]
    unnamed x13 -> x1, local copies, waits for them, and re-layouts: 36.9 us -> 1.61 us
    reduce_scatter x1 -> x0, waiting for transfers between devices: 27.4 us -> none  [on_device(): lax.psum_scatter(jnp.dot(act, down_weight, preferred_element_type=jnp.flo...]
    all_gather x1 -> x0, waiting for transfers between devices: 27.2 us -> none  [on_device(): gathered = lax.all_gather(blocks, 'gy', axis=0, tiled=True)]
    all_to_all x2 -> x0, blocking collectives: 20.9 us -> none  [the longest x1 11.9 us: on_device(): lax.all_to_all(stacked, 'gx', split_axis=2, concat_axis=0, tiled=True)]
    all_to_all x3 -> x0, local copies, waits for them, and re-layouts: 20 us -> none  [the longest x2 20 us: on_device(): lax.all_to_all(stacked, 'gx', split_axis=2, concat_axis=0, tiled=True)]
  transfers between devices with their start and end apart: 3 -> 0, of which waited for: 3 -> 0; matrix products, arithmetic and copies ran while one was open for 0% -> 0% of each run, Pallas kernels for 0% -> 0%
where the time goes in v1:
time: 90.4 us; the launch traced here: 90.2 us
  Pallas kernels  87.2 us (96%)
  local copies, waits for them, and re-layouts  3.03 us (3%)
    pallas_call x1, Pallas kernels, on_device(): pl.pallas_call(functools.partial(kernel, (X, Y, K, C, NC, SG, SD)), out_s...  87.2 us

profile of v1, /device:TPU:0, one launch (start us, length us, event | category | flops | bytes accessed | tf_op | source)
XLA Modules:
  0.0 90.2 jit_solution(6094901837616975383)
XLA Ops:
  0.0 1.4 %reshape.3.gain = bf16[1,16384]{1,0:T(2,128)(2,1)} reshape(bf16[16384]{0:T(1024)(128)(2,1)} %param.18) | data formatting | bytes 65536 | tf_op jit(solution)/shard_map/reshape | solution.py:389
  1.4 87.2 %layer.1 = bf16[4,16384]{1,0:T(4,128)(2,1)} custom-call(s32[4]{0:T(128)} %lengths.1, bf16[4,16384]{1,0:T(4,128)(2,1)} %resid.1, bf16[4,16384]{1,0:T(4,128)(2,1)} %query.1, bf16[4,1024]{1,0:T(4,128)(2,1)} %key_new.1, bf16[4,1024]{1,0:T(4,128)(2,1)} %value_new.1, bf16[1,16384]{1,0:T(2,128)(2,1)} %reshape.3.gain, bf16[4,128,1024]{2,1,0:T(8,128)(2,1)} %cache_keys.1, ...), custom_call_target="tpu_custom_call" | custom-call | tf_op jit(solution)/shard_map/layer/pallas_call | solution.py:373
  88.6 1.6 %copy.13 = bf16[4,16384]{1,0:T(4,128)(2,1)} copy(bf16[4,16384]{1,0:T(4,128)(2,1)} %layer.1) | data formatting | bytes 262144
